TPU v7x, 32 devices: a whole 2x2x4 slice. The times are simulated.
32 devices in a mesh: groups: 2 (over x), mset: 16 (over z, y, core).
Axes of the slice: x: 2, y: 2, z: 4, core: 2. Of those that a mesh axis runs over, the one named last changes fastest.
Arguments:
- m_list: int32 [16], replicated, may hold values from 1536 to 3071, as said below
- coeff: bfloat16 [32, 32, 1536], P(('groups', 'mset')), parts along dimension 0, may hold values from -6 to 6
- blocks: bfloat16 [32, 1536, 1536], P(('groups', 'mset')), parts along dimension 0, may hold values from -0.15625 to 0.15625
- legendre: bfloat16 [512, 16, 1536], P(('groups', 'mset')), parts along dimension 0, may hold values from -0.15625 to 0.15625
Outputs:
- sky_map: bfloat16 [512, 16, 8192], P(('groups', 'mset')), parts along dimension 0
There are 2 independent parts, one for each index of `groups`. A program takes and returns all parts, laid end to end along the dimension named above; an argument that names none is the same for every part. Nothing has to cross between parts.
Inputs may be any that keep to these rules, and one draw needn't show every extreme that they name: `m_list`: 16 distinct values; the value 3072 - 1536, a block of full order 1536, is always among them.
All inputs are finite; a program needn't handle non-finite values.
Results may differ from a plain program's by a relative error of at most 0.0062.
Values may be sent and summed in bfloat16 or wider, within the bound.
A program may use at most 64 MiB of HBM per device.

v0:
```python
import functools
import math

import jax
import jax.numpy as jnp
from jax import lax
from jax.experimental import pallas as pl
from jax.experimental.pallas import tpu as pltpu
from jax.sharding import PartitionSpec as P

LL = 3072
REAL = 16
NPHI = 8192
LANES = 128
MESH = pl.DeviceIdType.MESH
F32 = jnp.float32
BF16 = jnp.bfloat16


def iota(shape, dim):
    return lax.broadcasted_iota(jnp.int32, shape, dim)


def split_index(x, size):
    if size & (size - 1) == 0:
        shift = size.bit_length() - 1
        return lax.shift_right_logical(x, jnp.int32(shift)), lax.bitwise_and(x, jnp.int32(size - 1))
    quotient = x // size
    return quotient, x - quotient * size


def harmonics_kernel(
    n, chunks, m_ref, coeff_ref, blocks_ref, leg_ref, out_ref,
    coeff_v, blocks_v, leg_v, leg_away, leg_here, gathered, harm_away, harm,
    load_sem, recv_sem, up_sem, down_sem, sib_sem, leg_send, leg_recv, harm_sem,
):
    subset = m_ref.shape[0]
    cols, order_max = coeff_ref.shape[1], coeff_ref.shape[2]
    width = order_max // chunks
    group = 4
    depth = n // group
    line = 2 * depth
    rows_in = leg_ref.shape[0]
    rows_out = out_ref.shape[0]
    cycles = rows_in // subset
    rows_half = cycles * line
    span = line * cols
    me = lax.axis_index("mset")
    core = lax.rem(me, 2)
    side = lax.rem(lax.div(me, 2), 2)
    z = lax.div(me, group)
    sibling = me + 1 - 2 * core
    partner = me + 2 - 4 * side

    def load_block(q):
        return pltpu.make_async_copy(
            blocks_ref.at[0, :, pl.ds(q * width, width)], blocks_v.at[q], load_sem.at[q]
        )

    coeff_load = pltpu.make_async_copy(coeff_ref.at[0], coeff_v, load_sem.at[chunks])
    leg_load = pltpu.make_async_copy(leg_ref, leg_v, load_sem.at[chunks + 1])
    coeff_load.start()
    for q in range(chunks):
        load_block(q).start()
    leg_load.start()

    barrier = pltpu.get_barrier_semaphore()

    def greet(target):
        pl.semaphore_signal(barrier, inc=1, device_id={"mset": target}, device_id_type=MESH)

    greet(sibling)
    greet(partner)

    @pl.when(z > 0)
    def _():
        greet(me - group)

    @pl.when(z < depth - 1)
    def _():
        greet(me + group)

    def piece(pos, q):
        return gathered.at[q, pos]

    def copy(pos, q, target, send_sem):
        return pltpu.make_async_remote_copy(
            src_ref=piece(pos, q),
            dst_ref=piece(pos, q),
            send_sem=send_sem,
            recv_sem=recv_sem.at[q, pos],
            device_id={"mset": target},
            device_id_type=MESH,
        )

    def to_up(zz, q):
        return copy(2 * zz + core, q, me + group, up_sem.at[q, zz])

    def to_down(zz, q):
        return copy(2 * zz + core, q, me - group, down_sem.at[q, zz])

    def to_sib(zz, q):
        return copy(2 * zz + core, q, sibling, sib_sem.at[q, zz])

    def arrive(pos, q):
        copy(pos, q, sibling, sib_sem.at[q, 0]).wait_recv()

    def leg_copy(q):
        return pltpu.make_async_remote_copy(
            src_ref=leg_away.at[:, pl.ds(q * width, width)],
            dst_ref=leg_here.at[1, :, pl.ds(q * width, width)],
            send_sem=leg_send.at[q],
            recv_sem=leg_recv.at[q],
            device_id={"mset": partner},
            device_id_type=MESH,
        )

    def side_rows(which):
        row_cycle, row_pos = split_index(iota((rows_half, rows_in), 0), line)
        row_zz, row_core = split_index(row_pos, 2)
        wanted = row_cycle * subset + row_zz * group + which * 2 + row_core
        return jnp.where(iota((rows_half, rows_in), 1) == wanted, 1.0, 0.0).astype(BF16)

    order = LL - m_ref[me]
    coeff_load.wait()
    masked = jnp.where(iota((cols, order_max), 1) < order, coeff_v[...].astype(F32), 0.0).astype(BF16)
    for q in range(chunks):
        load_block(q).wait()
        product = jnp.dot(masked, blocks_v[q], preferred_element_type=F32)
        valid = iota((cols, width), 1) + q * width < order
        gathered[q, 2 * z + core] = jnp.where(valid, product, 0.0).astype(BF16)

        if q == 0:
            peers = 2 + jnp.where(z > 0, 1, 0) + jnp.where(z < depth - 1, 1, 0)
            pl.semaphore_wait(barrier, peers)

        @pl.when(z < depth - 1)
        def _():
            to_up(z, q).start()

        @pl.when(z > 0)
        def _():
            to_down(z, q).start()

        to_sib(z, q).start()

    away = side_rows(1 - side)
    leg_load.wait()
    for q in range(chunks):
        cut = slice(q * width, (q + 1) * width)
        leg_away[:, cut] = jnp.dot(away, leg_v[:, cut], preferred_element_type=F32).astype(BF16)
        leg_copy(q).start()

    here = side_rows(side)
    for q in range(chunks):
        cut = slice(q * width, (q + 1) * width)
        leg_here[0, :, cut] = jnp.dot(here, leg_v[:, cut], preferred_element_type=F32).astype(BF16)

    def below(d, q):
        arrive(2 * (z - d) + core, q)

        @pl.when(z < depth - 1)
        def _():
            to_up(z - d, q).start()

        to_sib(z - d, q).start()

    def above(d, q):
        arrive(2 * (z + d) + core, q)

        @pl.when(z > 0)
        def _():
            to_down(z + d, q).start()

        to_sib(z + d, q).start()

    for d in range(1, depth):
        for q in range(chunks):
            pl.when(z >= d)(functools.partial(below, d, q))
            pl.when(z <= depth - 1 - d)(functools.partial(above, d, q))
    for q in range(chunks):
        leg_copy(q).wait_recv()
    for zz in range(depth):
        for q in range(chunks):
            arrive(2 * zz + 1 - core, q)

    row_pos = split_index(iota((rows_half, span), 0), line)[1]
    same = row_pos == split_index(iota((rows_half, span), 1), cols)[0]
    gather_rows = jnp.where(
        iota((cycles, rows_half), 0) == split_index(iota((cycles, rows_half), 1), line)[0], 1.0, 0.0
    ).astype(BF16)

    def apply(which):
        cross = jnp.zeros((rows_half, span), F32)
        for q in range(chunks):
            cross += lax.dot_general(
                leg_here[which, :, q * width : (q + 1) * width],
                gathered[q].reshape(span, width),
                (((1,), (1,)), ((), ())),
                preferred_element_type=F32,
            )
        own = jnp.where(same, cross, 0.0).astype(BF16)
        return jnp.dot(gather_rows, own, preferred_element_type=F32).astype(BF16)

    harm_copy = pltpu.make_async_remote_copy(
        src_ref=harm_away,
        dst_ref=harm.at[side],
        send_sem=harm_sem.at[0],
        recv_sem=harm_sem.at[1],
        device_id={"mset": partner},
        device_id_type=MESH,
    )
    harm_away[...] = apply(1)
    harm_copy.start()
    harm[side] = apply(0)
    for zz in range(depth):
        for q in range(chunks):
            to_sib(zz, q).wait_send()

            @pl.when((z < depth - 1) & (zz <= z))
            def _():
                to_up(zz, q).wait_send()

            @pl.when((z > 0) & (zz >= z))
            def _():
                to_down(zz, q).wait_send()

    for q in range(chunks):
        leg_copy(q).wait_send()

    row_cycle, _ = split_index(iota((rows_out, cycles), 0), REAL)
    repeat = jnp.where(row_cycle == iota((rows_out, cycles), 1), 1.0, 0.0).astype(BF16)
    row_s = split_index(iota((rows_out, span), 0), REAL)[1]
    col_s = split_index(iota((rows_out, span), 1), REAL)[1]
    keep = row_s == col_s
    src_pos, src_c = split_index(iota((span, 2 * subset), 0), cols)
    src_zz, src_core = split_index(src_pos, 2)
    dst_part, dst_m = split_index(iota((span, 2 * subset), 1), subset)
    same_part = split_index(src_c, REAL)[0] == dst_part
    harm_copy.wait()
    total = jnp.zeros((rows_out, 2 * subset), F32)
    for which in range(2):
        spread = jnp.dot(repeat, harm[which], preferred_element_type=F32)
        picked = jnp.where(keep, spread, 0.0).astype(BF16)
        hit = same_part & (src_zz * group + which * 2 + src_core == dst_m)
        select = jnp.where(hit, 1.0, 0.0).astype(BF16)
        total += jnp.dot(picked, select, preferred_element_type=F32)
    out_ref[...] = total.astype(BF16)


def synthesis_kernel(tiles, scale, m_ref, h_v, out_ref, table, buf, sem):
    subset = m_ref.shape[0]
    tile = out_ref.shape[1] // tiles
    m_col = jnp.zeros((subset, LANES), jnp.int32)
    slot = iota((subset, LANES), 0)
    for i in range(subset):
        m_col = jnp.where(slot == i, m_ref[i], m_col)
    lane = iota((subset, LANES), 1)
    fine = split_index(m_col * lane, NPHI)[1].astype(F32) * (2.0 * math.pi / NPHI)
    coarse = split_index(m_col * (lane * LANES), NPHI)[1].astype(F32) * (2.0 * math.pi / NPHI)
    fine_cos, fine_sin = jnp.cos(fine), jnp.sin(fine)
    coarse_cos, coarse_sin = jnp.cos(coarse), jnp.sin(coarse)

    def fill(t):
        for a in range(t * tile // LANES, (t + 1) * tile // LANES):
            c = coarse_cos[:, a : a + 1]
            s = coarse_sin[:, a : a + 1]
            table[0:subset, a * LANES : (a + 1) * LANES] = (c * fine_cos - s * fine_sin).astype(BF16)
            table[subset : 2 * subset, a * LANES : (a + 1) * LANES] = (
                -(s * fine_cos + c * fine_sin)
            ).astype(BF16)

    copies = []
    fill(0)
    for t in range(tiles):
        cut = slice(t * tile, (t + 1) * tile)
        total = jnp.dot(h_v[...], table[:, cut], preferred_element_type=F32)
        buf[:, cut] = (total * scale).astype(BF16)
        copies.append(pltpu.make_async_copy(buf.at[:, cut], out_ref.at[:, cut], sem.at[t]))
        copies[-1].start()
        if t + 1 < tiles:
            fill(t + 1)
    for c in copies:
        c.wait()


def body(n, m_list, coeff, blocks, legendre):
    per_device, cols, order_max = coeff.shape
    assert per_device == 1 and n % 4 == 0
    cycles, subset, _ = legendre.shape
    chunks = 3
    depth = n // 4
    rows_in, rows_out = cycles * subset, cycles * REAL
    keep = functools.partial(pltpu.with_memory_space_constraint, memory_space=pltpu.HBM)
    vmem = pl.BlockSpec(memory_space=pltpu.VMEM)
    hbm = pl.BlockSpec(memory_space=pltpu.HBM)
    dma = pltpu.SemaphoreType.DMA
    harmonics = pl.pallas_call(
        functools.partial(harmonics_kernel, n, chunks),
        out_shape=jax.ShapeDtypeStruct((rows_out, 2 * subset), BF16),
        in_specs=[pl.BlockSpec(memory_space=pltpu.SMEM), hbm, hbm, hbm],
        out_specs=vmem,
        scratch_shapes=[
            pltpu.VMEM((cols, order_max), BF16),
            pltpu.VMEM((chunks, order_max, order_max // chunks), BF16),
            pltpu.VMEM((rows_in, order_max), BF16),
            pltpu.VMEM((rows_in // 2, order_max), BF16),
            pltpu.VMEM((2, rows_in // 2, order_max), BF16),
            pltpu.VMEM((chunks, n // 2, cols, order_max // chunks), BF16),
            pltpu.VMEM((cycles, n // 2 * cols), BF16),
            pltpu.VMEM((2, cycles, n // 2 * cols), BF16),
            dma((chunks + 2,)),
            dma((chunks, n // 2)),
            dma((chunks, depth)),
            dma((chunks, depth)),
            dma((chunks, depth)),
            dma((chunks,)),
            dma((chunks,)),
            dma((2,)),
        ],
        compiler_params=pltpu.CompilerParams(collective_id=0, has_side_effects=True, vmem_limit_bytes=40 << 20),
        name="harmonics",
    )(m_list, keep(coeff), keep(blocks), keep(legendre.reshape(rows_in, order_max)))
    tiles = 8
    sky = pl.pallas_call(
        functools.partial(synthesis_kernel, tiles, 1.0 / math.sqrt(subset)),
        out_shape=jax.ShapeDtypeStruct((rows_out, NPHI), BF16),
        in_specs=[pl.BlockSpec(memory_space=pltpu.SMEM), vmem],
        out_specs=hbm,
        scratch_shapes=[
            pltpu.VMEM((2 * subset, NPHI), BF16),
            pltpu.VMEM((rows_out, NPHI), BF16),
            dma((tiles,)),
        ],
        name="synthesis", compiler_params=pltpu.CompilerParams(vmem_limit_bytes=40 << 20),
    )(m_list, harmonics)
    return sky.reshape(cycles, REAL, NPHI)


def solution(mesh):
    spec = P(("groups", "mset"), None, None)
    return jax.shard_map(
        functools.partial(body, mesh.shape["mset"]),
        mesh=mesh,
        in_specs=(P(), spec, spec, spec),
        out_specs=spec,
        check_vma=False,
    )
```

profile of v0, /device:TPU:0, one launch (start us, length us, event | category | flops | bytes accessed | tf_op | source)
XLA Modules:
  0.0 23.9 jit_solution(12562117789910486519)
XLA Ops:
  0.0 0.0 copy-start
  0.0 0.7 %copy-done = s32[16]{0:T(128)S(1)} copy-done((s32[16]{0:T(128)S(1)}, s32[16]{0:T(128)}, u32[]{:S(2)}) %copy-start) | copy-done | bytes 88
  0.7 20.2 %harmonics.1.h_v = bf16[256,32]{1,0:T(8,128)(2,1)S(1)} custom-call(s32[16]{0:T(128)S(1)} %copy-done, bf16[1,32,1536]{2,1,0:T(8,128)(2,1)} %coeff_ref.1, bf16[1,1536,1536]{2,1,0:T(8,128)(2,1)} %blocks_ref.1, bf16[256,1536]{1,0:T(8,128)(2,1)} %bitcast.2), custom_call_target="tpu_custom_call" | custom-call | tf_op jit(solution)/shard_map/harmonics/pallas_call | solution.py:298
  20.8 3.1 %synthesis.1 = bf16[256,8192]{1,0:T(8,128)(2,1)} custom-call(s32[16]{0:T(128)S(1)} %copy-done, bf16[256,32]{1,0:T(8,128)(2,1)S(1)} %harmonics.1.h_v), custom_call_target="tpu_custom_call" | custom-call | tf_op jit(solution)/shard_map/synthesis/pallas_call | solution.py:325
Async XLA Ops:
  0.0 0.7 %copy-start = (s32[16]{0:T(128)S(1)}, s32[16]{0:T(128)}, u32[]{:S(2)}) copy-start(s32[16]{0:T(128)} %m_ref.3) | copy-start | bytes 196
where the time goes:
time: 24 us; the launch traced here: 23.9 us
  Pallas kernels  23.2 us (97%)
  local copies, waits for them, and re-layouts  0.65 us (3%)
    pallas_call x1, Pallas kernels, body(): pl.pallas_call(functools.partial(harmonics_kernel, n, chunks), out_shape=...  20.2 us
    pallas_call x1, Pallas kernels, body(): pl.pallas_call(functools.partial(synthesis_kernel, tiles, 1.0 / math.sqrt...  3.06 us
    unnamed x2, local copies, waits for them, and re-layouts  0.65 us

commit v1 on v0

v1 whole, which is shorter than its diff:
```python
import functools
import math

import jax
import jax.numpy as jnp
from jax import lax
from jax.experimental import pallas as pl
from jax.experimental.pallas import tpu as pltpu
from jax.sharding import PartitionSpec as P

LL = 3072
REAL = 16
NPHI = 8192
LANES = 128
MESH = pl.DeviceIdType.MESH
F32 = jnp.float32
BF16 = jnp.bfloat16


def iota(shape, dim):
    return lax.broadcasted_iota(jnp.int32, shape, dim)


def split_index(x, size):
    if size & (size - 1) == 0:
        shift = size.bit_length() - 1
        return lax.shift_right_logical(x, jnp.int32(shift)), lax.bitwise_and(x, jnp.int32(size - 1))
    quotient = x // size
    return quotient, x - quotient * size


def fill_table(m_s, table):
    subset = m_s.shape[0]
    m_col = jnp.zeros((subset, LANES), jnp.int32)
    slot = iota((subset, LANES), 0)
    for i in range(subset):
        m_col = jnp.where(slot == i, m_s[i], m_col)
    lane = iota((subset, LANES), 1)
    fine = split_index(m_col * lane, NPHI)[1].astype(F32) * (2.0 * math.pi / NPHI)
    coarse = split_index(m_col * (lane * LANES), NPHI)[1].astype(F32) * (2.0 * math.pi / NPHI)
    fine_cos, fine_sin = jnp.cos(fine), jnp.sin(fine)
    coarse_cos, coarse_sin = jnp.cos(coarse), jnp.sin(coarse)
    for a in range(NPHI // LANES):
        c = coarse_cos[:, a : a + 1]
        s = coarse_sin[:, a : a + 1]
        table[0:subset, a * LANES : (a + 1) * LANES] = (c * fine_cos - s * fine_sin).astype(BF16)
        table[subset : 2 * subset, a * LANES : (a + 1) * LANES] = (-(s * fine_cos + c * fine_sin)).astype(BF16)


def harmonics_kernel(
    n, chunks, m_ref, coeff_ref, blocks_ref, leg_ref, out_ref, table_ref,
    m_s, coeff_v, blocks_v, leg_v, leg_p, legs, legx, gathered, crossed, harm_s, harm_x, harm_r,
    load_sem, recv_sem, up_sem, down_sem, cross_send, cross_recv, next_send,
    sib_sem, zsib_sem, far_send, far_recv, quad_sem, turn_send, turn_recv, harm_send, harm_recv,
):
    subset = m_ref.shape[0]
    cols, order_max = coeff_ref.shape[1], coeff_ref.shape[2]
    width = order_max // chunks
    group = 4
    depth = n // group
    far = depth - 2
    rows_in = leg_ref.shape[0]
    rows_out = out_ref.shape[0]
    cycles = rows_in // subset
    span = depth * cols
    me = lax.axis_index("mset")
    core = lax.rem(me, 2)
    side = lax.rem(lax.div(me, 2), 2)
    z = lax.div(me, group)
    sibling = me + 1 - 2 * core
    partner = me + 2 - 4 * side
    diagonal = sibling + 2 - 4 * side
    odd = lax.rem(z, 2)
    mate_z = z + 1 - 2 * odd
    mate = me + group - 2 * group * odd
    mate_sib = sibling + group - 2 * group * odd
    upper = z >= depth // 2
    outer = jnp.where(upper, odd == 1, odd == 0)
    inner = jnp.logical_not(outer)
    pair_lo = z - odd

    def remote(src, dst, send_sem, recv_sem_, target):
        return pltpu.make_async_remote_copy(
            src_ref=src, dst_ref=dst, send_sem=send_sem, recv_sem=recv_sem_,
            device_id={"mset": target}, device_id_type=MESH,
        )

    def load_block(q):
        return pltpu.make_async_copy(
            blocks_ref.at[0, :, pl.ds(q * width, width)], blocks_v.at[q], load_sem.at[q]
        )

    m_load = pltpu.make_async_copy(m_ref, m_s, load_sem.at[chunks + 2])
    coeff_load = pltpu.make_async_copy(coeff_ref.at[0], coeff_v, load_sem.at[chunks])
    leg_load = pltpu.make_async_copy(leg_ref, leg_v, load_sem.at[chunks + 1])
    m_load.start()
    coeff_load.start()
    load_block(0).start()
    leg_load.start()
    for q in range(1, chunks):
        load_block(q).start()

    barrier = pltpu.get_barrier_semaphore()

    def greet(target):
        pl.semaphore_signal(barrier, inc=1, device_id={"mset": target}, device_id_type=MESH)

    greet(sibling)
    greet(partner)
    greet(diagonal)
    greet(mate_sib)

    @pl.when(z > 0)
    def _():
        greet(me - group)

    @pl.when(z < depth - 1)
    def _():
        greet(me + group)

    def to_up(zz, q):
        piece = gathered.at[q, zz]
        return remote(piece, piece, up_sem.at[q, zz], recv_sem.at[q, zz], me + group)

    def to_down(zz, q):
        piece = gathered.at[q, zz]
        return remote(piece, piece, down_sem.at[q, zz], recv_sem.at[q, zz], me - group)

    def arrive(zz, q):
        piece = gathered.at[q, zz]
        remote(piece, piece, up_sem.at[q, 0], recv_sem.at[q, zz], sibling).wait_recv()

    def to_cross(q):
        return remote(gathered.at[q, z], crossed.at[q, 0], cross_send.at[q], cross_recv.at[q, 0], partner)

    def to_next(q):
        return remote(crossed.at[q, 0], crossed.at[q, 1], next_send.at[q], cross_recv.at[q, 1], mate)

    leg_sib = remote(leg_p.at[0], legs.at[pl.ds(depth, depth)], sib_sem.at[0], sib_sem.at[1], sibling)
    leg_zsib = remote(leg_p.at[2, z], legx.at[0], zsib_sem.at[0], zsib_sem.at[1], sibling)

    def far_z(k):
        return k + jnp.where(k >= pair_lo, 2, 0)

    def leg_far(lane, k):
        target = diagonal if lane else partner
        return remote(
            leg_p.at[1 + lane, far_z(k)], legs.at[2 * depth + lane * far + k],
            far_send.at[lane, k], far_recv.at[lane, k], target,
        )

    leg_quad = remote(leg_p.at[1, mate_z], legx.at[1], quad_sem.at[0], quad_sem.at[1], mate)
    turn_slot = jnp.where(outer, 0, 1)
    leg_turn = remote(
        leg_p.at[2, mate_z], legx.at[2 + turn_slot], turn_send.at[0], turn_recv.at[turn_slot],
        jnp.where(outer, mate_sib, sibling),
    )

    m_load.wait()
    order = LL - m_s[me]
    coeff_load.wait()
    masked = jnp.where(iota((cols, order_max), 1) < order, coeff_v[...].astype(F32), 0.0).astype(BF16)

    def filter_chunk(q):
        load_block(q).wait()
        product = jnp.dot(masked, blocks_v[q], preferred_element_type=F32)
        valid = iota((cols, width), 1) + q * width < order
        gathered[q, z] = jnp.where(valid, product, 0.0).astype(BF16)

        if q == 0:
            peers = 4 + jnp.where(z > 0, 1, 0) + jnp.where(z < depth - 1, 1, 0)
            pl.semaphore_wait(barrier, peers)

        @pl.when(z < depth - 1)
        def _():
            to_up(z, q).start()

        @pl.when(z > 0)
        def _():
            to_down(z, q).start()

        to_cross(q).start()

    filter_chunk(0)

    rows_all = group * depth * cycles
    row_class, row_rest = split_index(iota((rows_all, rows_in), 0), depth * cycles)
    row_z, row_cycle = split_index(row_rest, cycles)
    row_dy, row_dc = split_index(row_class, 2)
    row_y = jnp.where(row_dy == 1, 1 - side, side)
    row_c = jnp.where(row_dc == 1, 1 - core, core)
    wanted = row_cycle * subset + row_z * group + row_y * 2 + row_c
    permute = jnp.where(iota((rows_all, rows_in), 1) == wanted, 1.0, 0.0).astype(BF16)
    leg_load.wait()
    for q in range(chunks):
        cut = slice(q * width, (q + 1) * width)
        moved = jnp.dot(permute, leg_v[:, cut], preferred_element_type=F32).astype(BF16)
        moved = moved.reshape(group, depth, cycles, width)
        legs[0:depth, :, cut] = moved[0]
        leg_p[:, :, :, cut] = moved[1:]

    for q in range(1, chunks):
        filter_chunk(q)

    for k in range(far):
        for lane in range(2):
            leg_far(lane, k).start()

    @pl.when(outer)
    def _():
        leg_quad.start()

    leg_turn.start()
    leg_sib.start()
    leg_zsib.start()

    fill_table(m_s, table_ref)

    def below(d, q):
        arrive(z - d, q)

        @pl.when(z < depth - 1)
        def _():
            to_up(z - d, q).start()

    def above(d, q):
        arrive(z + d, q)

        @pl.when(z > 0)
        def _():
            to_down(z + d, q).start()

    def cross_arrive(q):
        to_cross(q).wait_recv()

        @pl.when(outer)
        def _():
            to_next(q).start()

    def relay(d, q):
        pl.when(z >= d)(functools.partial(below, d, q))
        pl.when(z <= depth - 1 - d)(functools.partial(above, d, q))

    for d in range(1, depth - 1):
        for q in range(chunks):
            relay(d, q)
            if d == 1:
                cross_arrive(q)

    lane_z = split_index(iota((cycles, span), 1), cols)[0]

    def at_z(x, zz):
        return jnp.where(lane_z == zz, x, 0.0)

    contract_last = (((1,), (1,)), ((), ()))

    def meet(rows, slot):
        total = jnp.zeros((rows.shape[0], span), F32)
        for q in range(chunks):
            f = crossed[q, slot]
            total += lax.dot_general(
                rows[:, q * width : (q + 1) * width], jnp.concatenate([f] * depth, axis=0),
                contract_last, preferred_element_type=F32,
            )
        return total

    def harm_copy(src, slot, target):
        return remote(src, harm_r.at[slot], harm_send.at[slot], harm_recv.at[slot], target)

    to_sib = harm_copy(harm_s.at[0], 0, sibling)
    to_partner = harm_copy(harm_s.at[1], 1, partner)
    to_diag = harm_copy(harm_s.at[2], 2, diagonal)
    to_sib_x = harm_copy(harm_x.at[1], 3, sibling)
    to_mate = harm_copy(harm_x.at[2], 4, mate)
    to_mate_sib = harm_copy(harm_x.at[3], 5, mate_sib)

    leg_zsib.wait_recv()

    @pl.when(outer)
    def _():
        x = meet(jnp.concatenate([leg_p[1, z], legx[0]], axis=0), 0)
        harm_x[0] = at_z(x[0:cycles], z).astype(BF16)
        harm_x[1] = at_z(x[cycles : 2 * cycles], z).astype(BF16)
        to_sib_x.start()

    leg_sib.wait_recv()
    total_rows = (2 * depth + 2 * far) * cycles
    cross = jnp.zeros((total_rows, span), F32)
    for q in range(chunks):
        relay(depth - 1, q)
        if q == 0:
            for k in range(far):
                for lane in range(2):
                    leg_far(lane, k).wait_recv()
        cross += lax.dot_general(
            legs[:, :, q * width : (q + 1) * width].reshape(total_rows, width),
            gathered[q].reshape(span, width),
            contract_last, preferred_element_type=F32,
        )

    def collect(first, zs):
        out = jnp.zeros((cycles, span), F32)
        for k, zz in enumerate(zs):
            out += at_z(cross[(first + k) * cycles : (first + k + 1) * cycles], zz)
        return out.astype(BF16)

    far_list = [far_z(k) for k in range(far)]
    harm_s[1] = collect(2 * depth, far_list)
    to_partner.start()
    harm_s[2] = collect(2 * depth + far, far_list)
    to_diag.start()
    harm_s[0] = collect(depth, range(depth))
    to_sib.start()
    own = collect(0, range(depth))

    @pl.when(inner)
    def _():
        leg_quad.wait_recv()
        for slot in range(2):
            remote(leg_p.at[2, mate_z], legx.at[2 + slot], turn_send.at[0], turn_recv.at[slot], sibling).wait_recv()
        x = meet(jnp.concatenate([leg_p[1, z], legx[0], legx[1], legx[2]], axis=0), 0)
        harm_x[2] = at_z(x[2 * cycles : 3 * cycles], z).astype(BF16)
        to_mate.start()
        harm_x[3] = at_z(x[3 * cycles : 4 * cycles], z).astype(BF16)
        to_mate_sib.start()
        for q in range(chunks):
            to_next(q).wait_recv()
        w = meet(jnp.concatenate([leg_p[1, mate_z], legx[3]], axis=0), 1)
        harm_x[1] = (at_z(x[cycles : 2 * cycles], z) + at_z(w[cycles : 2 * cycles], mate_z)).astype(BF16)
        to_sib_x.start()
        harm_x[0] = (at_z(x[0:cycles], z) + at_z(w[0:cycles], mate_z)).astype(BF16)
        harm_r[4] = jnp.zeros((cycles, span), BF16)
        harm_r[5] = jnp.zeros((cycles, span), BF16)

    for zz in range(depth):
        for q in range(chunks):

            @pl.when((z < depth - 1) & (zz <= z))
            def _():
                to_up(zz, q).wait_send()

            @pl.when((z > 0) & (zz >= z))
            def _():
                to_down(zz, q).wait_send()

    for q in range(chunks):
        to_cross(q).wait_send()
    for k in range(far):
        for lane in range(2):
            leg_far(lane, k).wait_send()
    leg_sib.wait_send()
    leg_zsib.wait_send()
    leg_turn.wait_send()

    @pl.when(outer)
    def _():
        for q in range(chunks):
            to_next(q).wait_send()
        leg_quad.wait_send()

    @pl.when(inner)
    def _():
        to_mate.wait_send()
        to_mate_sib.wait_send()

    rows_cycle, rows_s = split_index(iota((rows_out, cycles), 0), REAL)
    repeat = jnp.where(rows_cycle == iota((rows_out, cycles), 1), 1.0, 0.0).astype(BF16)
    wide = group * span
    keep = split_index(iota((rows_out, wide), 0), REAL)[1] == split_index(iota((rows_out, wide), 1), REAL)[1]
    src_class, src_rest = split_index(iota((wide, 2 * subset), 0), span)
    src_z, src_c = split_index(src_rest, cols)
    src_dy, src_dc = split_index(src_class, 2)
    src_y = jnp.where(src_dy == 1, 1 - side, side)
    src_core = jnp.where(src_dc == 1, 1 - core, core)
    dst_part, dst_m = split_index(iota((wide, 2 * subset), 1), subset)
    hit = (split_index(src_c, REAL)[0] == dst_part) & (src_z * group + src_y * 2 + src_core == dst_m)
    select = jnp.where(hit, 1.0, 0.0).astype(BF16)

    to_sib_x.wait()

    @pl.when(outer)
    def _():
        to_mate.wait_recv()
        to_mate_sib.wait_recv()

    to_sib.wait()
    to_partner.wait()
    to_diag.wait()
    near = harm_x[0] + harm_r[1] + harm_r[4]
    away = harm_r[3] + harm_r[2] + harm_r[5]
    everything = jnp.concatenate([own, harm_r[0], near, away], axis=1)
    spread = jnp.dot(repeat, everything, preferred_element_type=F32)
    picked = jnp.where(keep, spread, 0.0).astype(BF16)
    out_ref[...] = jnp.dot(picked, select, preferred_element_type=F32).astype(BF16)


def synthesis_kernel(tiles, scale, h_v, table, out_ref, buf, sem):
    tile = out_ref.shape[1] // tiles
    copies = []
    for t in range(tiles):
        cut = slice(t * tile, (t + 1) * tile)
        total = jnp.dot(h_v[...], table[:, cut], preferred_element_type=F32)
        buf[:, cut] = (total * scale).astype(BF16)
        copies.append(pltpu.make_async_copy(buf.at[:, cut], out_ref.at[:, cut], sem.at[t]))
        copies[-1].start()
    for c in copies:
        c.wait()


def body(n, m_list, coeff, blocks, legendre):
    per_device, cols, order_max = coeff.shape
    assert per_device == 1 and n % 8 == 0
    cycles, subset, _ = legendre.shape
    chunks = 3
    depth = n // 4
    far = depth - 2
    width = order_max // chunks
    span = depth * cols
    rows_in, rows_out = cycles * subset, cycles * REAL
    keep = functools.partial(pltpu.with_memory_space_constraint, memory_space=pltpu.HBM)
    vmem = pl.BlockSpec(memory_space=pltpu.VMEM)
    hbm = pl.BlockSpec(memory_space=pltpu.HBM)
    dma = pltpu.SemaphoreType.DMA
    harmonics, table = pl.pallas_call(
        functools.partial(harmonics_kernel, n, chunks),
        out_shape=(
            jax.ShapeDtypeStruct((rows_out, 2 * subset), BF16),
            jax.ShapeDtypeStruct((2 * subset, NPHI), BF16),
        ),
        in_specs=[hbm, hbm, hbm, hbm],
        out_specs=(vmem, vmem),
        scratch_shapes=[
            pltpu.SMEM((subset,), jnp.int32),
            pltpu.VMEM((cols, order_max), BF16),
            pltpu.VMEM((chunks, order_max, width), BF16),
            pltpu.VMEM((rows_in, order_max), BF16),
            pltpu.VMEM((3, depth, cycles, order_max), BF16),
            pltpu.VMEM((2 * depth + 2 * far, cycles, order_max), BF16),
            pltpu.VMEM((4, cycles, order_max), BF16),
            pltpu.VMEM((chunks, depth, cols, width), BF16),
            pltpu.VMEM((chunks, 2, cols, width), BF16),
            pltpu.VMEM((3, cycles, span), BF16),
            pltpu.VMEM((4, cycles, span), BF16),
            pltpu.VMEM((6, cycles, span), BF16),
            dma((chunks + 3,)),
            dma((chunks, depth)),
            dma((chunks, depth)),
            dma((chunks, depth)),
            dma((chunks,)),
            dma((chunks, 2)),
            dma((chunks,)),
            dma((2,)),
            dma((2,)),
            dma((2, far)),
            dma((2, far)),
            dma((2,)),
            dma((1,)),
            dma((2,)),
            dma((6,)),
            dma((6,)),
        ],
        compiler_params=pltpu.CompilerParams(collective_id=0, has_side_effects=True, vmem_limit_bytes=40 << 20),
        name="harmonics",
    )(keep(m_list), keep(coeff), keep(blocks), keep(legendre.reshape(rows_in, order_max)))
    tiles = 8
    sky = pl.pallas_call(
        functools.partial(synthesis_kernel, tiles, 1.0 / math.sqrt(subset)),
        out_shape=jax.ShapeDtypeStruct((rows_out, NPHI), BF16),
        in_specs=[vmem, vmem],
        out_specs=hbm,
        scratch_shapes=[
            pltpu.VMEM((rows_out, NPHI), BF16),
            dma((tiles,)),
        ],
        name="synthesis", compiler_params=pltpu.CompilerParams(vmem_limit_bytes=40 << 20),
    )(harmonics, table)
    return sky.reshape(cycles, REAL, NPHI)


def solution(mesh):
    spec = P(("groups", "mset"), None, None)
    return jax.shard_map(
        functools.partial(body, mesh.shape["mset"]),
        mesh=mesh,
        in_specs=(P(), spec, spec, spec),
        out_specs=spec,
        check_vma=False,
    )
```

time: 24 us -> 22.5 us (0.938)
  Pallas kernels: 23.2 us -> 22.3 us
  local copies, waits for them, and re-layouts: 0.65 us -> 0 us
    pallas_call x1, Pallas kernels: 3.06 us -> 2.34 us  [body(): pl.pallas_call(functools.partial(synthesis_kernel, tiles, 1.0 / math.sqrt...]
    unnamed x2 -> x0, local copies, waits for them, and re-layouts: 0.65 us -> none
where the time goes in v1:
time: 22.5 us; the launch traced here: 22.3 us
  Pallas kernels  22.3 us (99%)
    pallas_call x1, Pallas kernels, body(): pl.pallas_call(functools.partial(harmonics_kernel, n, chunks), out_shape=...  20 us
    pallas_call x1, Pallas kernels, body(): pl.pallas_call(functools.partial(synthesis_kernel, tiles, 1.0 / math.sqrt...  2.34 us

profile of v1, /device:TPU:0, one launch (start us, length us, event | category | flops | bytes accessed | tf_op | source)
XLA Modules:
  0.0 22.3 jit_solution(16190484196771819466)
XLA Ops:
  0.0 20.0 %harmonics.1 = (bf16[256,32]{1,0:T(8,128)(2,1)S(1)}, bf16[32,8192]{1,0:T(8,128)(2,1)S(1)}) custom-call(s32[16]{0:T(128)} %m_ref.1, bf16[1,32,1536]{2,1,0:T(8,128)(2,1)} %coeff_ref.1, bf16[1,1536,1536]{2,1,0:T(8,128)(2,1)} %blocks_ref.1, bf16[256,1536]{1,0:T(8,128)(2,1)} %bitcast.2), custom_call_target="tpu_custom_call" | custom-call | tf_op jit(solution)/shard_map/harmonics/pallas_call | solution.py:424
  20.0 2.3 %synthesis.1 = bf16[256,8192]{1,0:T(8,128)(2,1)} custom-call(bf16[256,32]{1,0:T(8,128)(2,1)S(1)} %get-tuple-element.7.h_v, bf16[32,8192]{1,0:T(8,128)(2,1)S(1)} %get-tuple-element.8.table), custom_call_target="tpu_custom_call" | custom-call | tf_op jit(solution)/shard_map/synthesis/pallas_call | solution.py:466

commit v2 on v1

--- a/solution.py
+++ b/solution.py
@@ -15,6 +15,7 @@
 MESH = pl.DeviceIdType.MESH
 F32 = jnp.float32
 BF16 = jnp.bfloat16
+CHUNKS = 3
 
 
 def iota(shape, dim):
@@ -50,8 +51,8 @@
 def harmonics_kernel(
     n, chunks, m_ref, coeff_ref, blocks_ref, leg_ref, out_ref, table_ref,
     m_s, coeff_v, blocks_v, leg_v, leg_p, legs, legx, gathered, crossed, harm_s, harm_x, harm_r,
-    load_sem, recv_sem, up_sem, down_sem, cross_send, cross_recv, next_send,
-    sib_sem, zsib_sem, far_send, far_recv, quad_sem, turn_send, turn_recv, harm_send, harm_recv,
+    load_sem, recv_sem, up_sem, down_sem, end_send, cross_send, cross_recv, next_send,
+    sib_sem, zsib_sem, far_send, far_recv, quad_sem, low_send, low_recv, turn_send, turn_recv, harm_send, harm_recv,
 ):
     subset = m_ref.shape[0]
     cols, order_max = coeff_ref.shape[1], coeff_ref.shape[2]
@@ -95,10 +96,9 @@
     leg_load = pltpu.make_async_copy(leg_ref, leg_v, load_sem.at[chunks + 1])
     m_load.start()
     coeff_load.start()
-    load_block(0).start()
+    for q in range(chunks):
+        load_block(q).start()
     leg_load.start()
-    for q in range(1, chunks):
-        load_block(q).start()
 
     barrier = pltpu.get_barrier_semaphore()
 
@@ -110,6 +110,10 @@
     greet(diagonal)
     greet(mate_sib)
 
+    @pl.when(z == 0)
+    def _():
+        greet(me + (depth - 1) * group)
+
     @pl.when(z > 0)
     def _():
         greet(me - group)
@@ -125,6 +129,10 @@
     def to_down(zz, q):
         piece = gathered.at[q, zz]
         return remote(piece, piece, down_sem.at[q, zz], recv_sem.at[q, zz], me - group)
+
+    def to_end(q):
+        piece = gathered.at[q, depth - 1]
+        return remote(piece, piece, end_send.at[q], recv_sem.at[q, depth - 1], me - (depth - 1) * group)
 
     def arrive(zz, q):
         piece = gathered.at[q, zz]
@@ -156,6 +164,9 @@
         jnp.where(outer, mate_sib, sibling),
     )
 
+    leg_low = remote(legs.at[1], legx.at[4], low_send.at[0], low_recv.at[0], mate)
+    leg_low_sib = remote(leg_p.at[0, 1], legx.at[5], low_send.at[1], low_recv.at[1], mate_sib)
+
     m_load.wait()
     order = LL - m_s[me]
     coeff_load.wait()
@@ -168,20 +179,25 @@
         gathered[q, z] = jnp.where(valid, product, 0.0).astype(BF16)
 
         if q == 0:
-            peers = 4 + jnp.where(z > 0, 1, 0) + jnp.where(z < depth - 1, 1, 0)
+            peers = 4 + jnp.where(z > 0, 1, 0) + jnp.where(z < depth - 1, 1, 1)
             pl.semaphore_wait(barrier, peers)
+
+        @pl.when(z == depth - 1)
+        def _():
+            to_end(q).start()
 
         @pl.when(z < depth - 1)
         def _():
             to_up(z, q).start()
 
-        @pl.when(z > 0)
+        @pl.when(z > 1)
         def _():
             to_down(z, q).start()
 
         to_cross(q).start()
 
-    filter_chunk(0)
+    for q in range(chunks):
+        filter_chunk(q)
 
     rows_all = group * depth * cycles
     row_class, row_rest = split_index(iota((rows_all, rows_in), 0), depth * cycles)
@@ -199,9 +215,6 @@
         legs[0:depth, :, cut] = moved[0]
         leg_p[:, :, :, cut] = moved[1:]
 
-    for q in range(1, chunks):
-        filter_chunk(q)
-
     for k in range(far):
         for lane in range(2):
             leg_far(lane, k).start()
@@ -211,6 +224,12 @@
         leg_quad.start()
 
     leg_turn.start()
+
+    @pl.when(z == 0)
+    def _():
+        leg_low.start()
+        leg_low_sib.start()
+
     leg_sib.start()
     leg_zsib.start()
 
@@ -225,10 +244,11 @@
 
     def above(d, q):
         arrive(z + d, q)
-
-        @pl.when(z > 0)
-        def _():
-            to_down(z + d, q).start()
+        if d < depth - 2:
+
+            @pl.when(z > 0)
+            def _():
+                to_down(z + d, q).start()
 
     def cross_arrive(q):
         to_cross(q).wait_recv()
@@ -239,7 +259,7 @@
 
     def relay(d, q):
         pl.when(z >= d)(functools.partial(below, d, q))
-        pl.when(z <= depth - 1 - d)(functools.partial(above, d, q))
+        pl.when((z <= depth - 1 - d) & (z > (0 if d == 1 else -1)))(functools.partial(above, d, q))
 
     for d in range(1, depth - 1):
         for q in range(chunks):
@@ -254,10 +274,10 @@
 
     contract_last = (((1,), (1,)), ((), ()))
 
-    def meet(rows, slot):
+    def meet(rows, block):
         total = jnp.zeros((rows.shape[0], span), F32)
         for q in range(chunks):
-            f = crossed[q, slot]
+            f = block(q)
             total += lax.dot_general(
                 rows[:, q * width : (q + 1) * width], jnp.concatenate([f] * depth, axis=0),
                 contract_last, preferred_element_type=F32,
@@ -265,23 +285,54 @@
         return total
 
     def harm_copy(src, slot, target):
-        return remote(src, harm_r.at[slot], harm_send.at[slot], harm_recv.at[slot], target)
+        dst = harm_r.at[slot] if slot < 4 else harm_r.at[pl.ds(2 * slot - 4, 2)]
+        return remote(src, dst, harm_send.at[slot], harm_recv.at[slot], target)
 
     to_sib = harm_copy(harm_s.at[0], 0, sibling)
     to_partner = harm_copy(harm_s.at[1], 1, partner)
     to_diag = harm_copy(harm_s.at[2], 2, diagonal)
     to_sib_x = harm_copy(harm_x.at[1], 3, sibling)
-    to_mate = harm_copy(harm_x.at[2], 4, mate)
-    to_mate_sib = harm_copy(harm_x.at[3], 5, mate_sib)
+    to_mate = harm_copy(harm_x.at[pl.ds(2, 2)], 4, mate)
+    to_mate_sib = harm_copy(harm_x.at[pl.ds(4, 2)], 5, mate_sib)
 
     leg_zsib.wait_recv()
 
     @pl.when(outer)
     def _():
-        x = meet(jnp.concatenate([leg_p[1, z], legx[0]], axis=0), 0)
+        x = meet(jnp.concatenate([leg_p[1, z], legx[0]], axis=0), lambda q: crossed[q, 0])
         harm_x[0] = at_z(x[0:cycles], z).astype(BF16)
         harm_x[1] = at_z(x[cycles : 2 * cycles], z).astype(BF16)
         to_sib_x.start()
+
+    @pl.when(inner)
+    def _():
+        leg_quad.wait_recv()
+        remote(leg_p.at[2, mate_z], legx.at[2], turn_send.at[0], turn_recv.at[0], sibling).wait_recv()
+        x = meet(jnp.concatenate([leg_p[1, z], legx[0], legx[1], legx[2]], axis=0), lambda q: crossed[q, 0])
+        harm_x[0] = at_z(x[0:cycles], z).astype(BF16)
+        harm_x[1] = at_z(x[cycles : 2 * cycles], z).astype(BF16)
+        harm_x[2] = at_z(x[2 * cycles : 3 * cycles], z).astype(BF16)
+        harm_x[4] = at_z(x[3 * cycles : 4 * cycles], z).astype(BF16)
+        harm_x[3] = jnp.zeros((cycles, span), BF16)
+        harm_x[5] = jnp.zeros((cycles, span), BF16)
+        harm_r[4:8] = jnp.zeros((4, cycles, span), BF16)
+
+    @pl.when(z == 1)
+    def _():
+        leg_low.wait_recv()
+        leg_low_sib.wait_recv()
+        x = meet(jnp.concatenate([legx[4], legx[5]], axis=0), lambda q: gathered[q, z])
+        harm_x[3] = at_z(x[0:cycles], z).astype(BF16)
+        harm_x[5] = at_z(x[cycles : 2 * cycles], z).astype(BF16)
+
+    @pl.when(inner)
+    def _():
+        to_mate.start()
+        to_mate_sib.start()
+
+    @pl.when(z == 0)
+    def _():
+        gathered[:, 1] = jnp.zeros((chunks, cols, width), BF16)
 
     leg_sib.wait_recv()
     total_rows = (2 * depth + 2 * far) * cycles
@@ -315,22 +366,13 @@
 
     @pl.when(inner)
     def _():
-        leg_quad.wait_recv()
-        for slot in range(2):
-            remote(leg_p.at[2, mate_z], legx.at[2 + slot], turn_send.at[0], turn_recv.at[slot], sibling).wait_recv()
-        x = meet(jnp.concatenate([leg_p[1, z], legx[0], legx[1], legx[2]], axis=0), 0)
-        harm_x[2] = at_z(x[2 * cycles : 3 * cycles], z).astype(BF16)
-        to_mate.start()
-        harm_x[3] = at_z(x[3 * cycles : 4 * cycles], z).astype(BF16)
-        to_mate_sib.start()
         for q in range(chunks):
             to_next(q).wait_recv()
-        w = meet(jnp.concatenate([leg_p[1, mate_z], legx[3]], axis=0), 1)
-        harm_x[1] = (at_z(x[cycles : 2 * cycles], z) + at_z(w[cycles : 2 * cycles], mate_z)).astype(BF16)
+        remote(leg_p.at[2, mate_z], legx.at[3], turn_send.at[0], turn_recv.at[1], sibling).wait_recv()
+        w = meet(jnp.concatenate([leg_p[1, mate_z], legx[3]], axis=0), lambda q: crossed[q, 1])
+        harm_x[1] = harm_x[1] + at_z(w[cycles : 2 * cycles], mate_z).astype(BF16)
         to_sib_x.start()
-        harm_x[0] = (at_z(x[0:cycles], z) + at_z(w[0:cycles], mate_z)).astype(BF16)
-        harm_r[4] = jnp.zeros((cycles, span), BF16)
-        harm_r[5] = jnp.zeros((cycles, span), BF16)
+        harm_x[0] = harm_x[0] + at_z(w[0:cycles], mate_z).astype(BF16)
 
     for zz in range(depth):
         for q in range(chunks):
@@ -339,12 +381,17 @@
             def _():
                 to_up(zz, q).wait_send()
 
-            @pl.when((z > 0) & (zz >= z))
+            @pl.when((z > (1 if zz in (1, depth - 1) else 0)) & (zz >= z))
             def _():
                 to_down(zz, q).wait_send()
 
     for q in range(chunks):
         to_cross(q).wait_send()
+
+        @pl.when(z == depth - 1)
+        def _():
+            to_end(q).wait_send()
+
     for k in range(far):
         for lane in range(2):
             leg_far(lane, k).wait_send()
@@ -357,6 +404,11 @@
         for q in range(chunks):
             to_next(q).wait_send()
         leg_quad.wait_send()
+
+    @pl.when(z == 0)
+    def _():
+        leg_low.wait_send()
+        leg_low_sib.wait_send()
 
     @pl.when(inner)
     def _():
@@ -387,8 +439,8 @@
     to_partner.wait()
     to_diag.wait()
     near = harm_x[0] + harm_r[1] + harm_r[4]
-    away = harm_r[3] + harm_r[2] + harm_r[5]
-    everything = jnp.concatenate([own, harm_r[0], near, away], axis=1)
+    away = harm_r[3] + harm_r[2] + harm_r[6]
+    everything = jnp.concatenate([own + harm_r[5], harm_r[0] + harm_r[7], near, away], axis=1)
     spread = jnp.dot(repeat, everything, preferred_element_type=F32)
     picked = jnp.where(keep, spread, 0.0).astype(BF16)
     out_ref[...] = jnp.dot(picked, select, preferred_element_type=F32).astype(BF16)
@@ -409,9 +461,9 @@
 
 def body(n, m_list, coeff, blocks, legendre):
     per_device, cols, order_max = coeff.shape
-    assert per_device == 1 and n % 8 == 0
+    assert per_device == 1 and n % 16 == 0 and order_max % (CHUNKS * LANES) == 0
     cycles, subset, _ = legendre.shape
-    chunks = 3
+    chunks = CHUNKS
     depth = n // 4
     far = depth - 2
     width = order_max // chunks
@@ -436,16 +488,17 @@
             pltpu.VMEM((rows_in, order_max), BF16),
             pltpu.VMEM((3, depth, cycles, order_max), BF16),
             pltpu.VMEM((2 * depth + 2 * far, cycles, order_max), BF16),
-            pltpu.VMEM((4, cycles, order_max), BF16),
+            pltpu.VMEM((6, cycles, order_max), BF16),
             pltpu.VMEM((chunks, depth, cols, width), BF16),
             pltpu.VMEM((chunks, 2, cols, width), BF16),
             pltpu.VMEM((3, cycles, span), BF16),
-            pltpu.VMEM((4, cycles, span), BF16),
             pltpu.VMEM((6, cycles, span), BF16),
+            pltpu.VMEM((8, cycles, span), BF16),
             dma((chunks + 3,)),
             dma((chunks, depth)),
             dma((chunks, depth)),
             dma((chunks, depth)),
+            dma((chunks,)),
             dma((chunks,)),
             dma((chunks, 2)),
             dma((chunks,)),
@@ -453,6 +506,8 @@
             dma((2,)),
             dma((2, far)),
             dma((2, far)),
+            dma((2,)),
+            dma((2,)),
             dma((2,)),
             dma((1,)),
             dma((2,)),

time: 22.5 us -> 21.5 us (0.956)
  Pallas kernels: 22.3 us -> 21.3 us
    pallas_call x1, Pallas kernels: 20 us -> 19 us  [body(): pl.pallas_call(functools.partial(harmonics_kernel, n, chunks), out_shape=...]
where the time goes in v2:
time: 21.5 us; the launch traced here: 21.3 us
  Pallas kernels  21.3 us (99%)
    pallas_call x1, Pallas kernels, body(): pl.pallas_call(functools.partial(harmonics_kernel, n, chunks), out_shape=...  19 us
    pallas_call x1, Pallas kernels, body(): pl.pallas_call(functools.partial(synthesis_kernel, tiles, 1.0 / math.sqrt...  2.35 us

profile of v2, /device:TPU:0, one launch (start us, length us, event | category | flops | bytes accessed | tf_op | source)
XLA Modules:
  0.0 21.3 jit_solution(14273656181240461078)
XLA Ops:
  0.0 19.0 %harmonics.1 = (bf16[256,32]{1,0:T(8,128)(2,1)S(1)}, bf16[32,8192]{1,0:T(8,128)(2,1)S(1)}) custom-call(s32[16]{0:T(128)} %m_ref.1, bf16[1,32,1536]{2,1,0:T(8,128)(2,1)} %coeff_ref.1, bf16[1,1536,1536]{2,1,0:T(8,128)(2,1)} %blocks_ref.1, bf16[256,1536]{1,0:T(8,128)(2,1)} %bitcast.2), custom_call_target="tpu_custom_call" | custom-call | tf_op jit(solution)/shard_map/harmonics/pallas_call | solution.py:476
  19.0 2.3 %synthesis.1 = bf16[256,8192]{1,0:T(8,128)(2,1)} custom-call(bf16[256,32]{1,0:T(8,128)(2,1)S(1)} %get-tuple-element.7.h_v, bf16[32,8192]{1,0:T(8,128)(2,1)S(1)} %get-tuple-element.8.table), custom_call_target="tpu_custom_call" | custom-call | tf_op jit(solution)/shard_map/synthesis/pallas_call | solution.py:521

commit v3 on v2

--- a/solution.py
+++ b/solution.py
@@ -199,6 +199,7 @@
     for q in range(chunks):
         filter_chunk(q)
 
+
     rows_all = group * depth * cycles
     row_class, row_rest = split_index(iota((rows_all, rows_in), 0), depth * cycles)
     row_z, row_cycle = split_index(row_rest, cycles)
@@ -237,35 +238,28 @@
 
     def below(d, q):
         arrive(z - d, q)
-
-        @pl.when(z < depth - 1)
-        def _():
-            to_up(z - d, q).start()
+        to_up(z - d, q).start()
 
     def above(d, q):
         arrive(z + d, q)
-        if d < depth - 2:
-
-            @pl.when(z > 0)
-            def _():
-                to_down(z + d, q).start()
-
-    def cross_arrive(q):
-        to_cross(q).wait_recv()
-
-        @pl.when(outer)
-        def _():
+        to_down(z + d, q).start()
+
+    def take(zz, q):
+        arrive(zz, q)
+
+    for d in range(1, depth - 1):
+        for q in range(chunks):
+            pl.when((z >= d) & (z < depth - 1))(functools.partial(below, d, q))
+
+    @pl.when(outer)
+    def _():
+        for q in range(chunks):
+            to_cross(q).wait_recv()
             to_next(q).start()
 
-    def relay(d, q):
-        pl.when(z >= d)(functools.partial(below, d, q))
-        pl.when((z <= depth - 1 - d) & (z > (0 if d == 1 else -1)))(functools.partial(above, d, q))
-
     for d in range(1, depth - 1):
         for q in range(chunks):
-            relay(d, q)
-            if d == 1:
-                cross_arrive(q)
+            pl.when((z <= depth - 1 - d) & (z > (1 if d == depth - 2 else 0)))(functools.partial(above, d, q))
 
     lane_z = split_index(iota((cycles, span), 1), cols)[0]
 
@@ -306,6 +300,8 @@
 
     @pl.when(inner)
     def _():
+        for q in range(chunks):
+            to_cross(q).wait_recv()
         leg_quad.wait_recv()
         remote(leg_p.at[2, mate_z], legx.at[2], turn_send.at[0], turn_recv.at[0], sibling).wait_recv()
         x = meet(jnp.concatenate([leg_p[1, z], legx[0], legx[1], legx[2]], axis=0), lambda q: crossed[q, 0])
@@ -338,7 +334,11 @@
     total_rows = (2 * depth + 2 * far) * cycles
     cross = jnp.zeros((total_rows, span), F32)
     for q in range(chunks):
-        relay(depth - 1, q)
+        pl.when(z == 1)(functools.partial(take, depth - 1, q))
+        for d in range(1, depth):
+            if d > 1:
+                pl.when(z == 0)(functools.partial(take, d, q))
+            pl.when(z == depth - 1)(functools.partial(take, depth - 1 - d, q))
         if q == 0:
             for k in range(far):
                 for lane in range(2):

time: 21.5 us -> 20 us (0.930)
  Pallas kernels: 21.3 us -> 19.9 us
    pallas_call x1, Pallas kernels: 19 us -> 17.5 us  [body(): pl.pallas_call(functools.partial(harmonics_kernel, n, chunks), out_shape=...]
where the time goes in v3:
time: 20 us; the launch traced here: 19.9 us
  Pallas kernels  19.9 us (99%)
    pallas_call x1, Pallas kernels, body(): pl.pallas_call(functools.partial(harmonics_kernel, n, chunks), out_shape=...  17.5 us
    pallas_call x1, Pallas kernels, body(): pl.pallas_call(functools.partial(synthesis_kernel, tiles, 1.0 / math.sqrt...  2.35 us

profile of v3, /device:TPU:0, one launch (start us, length us, event | category | flops | bytes accessed | tf_op | source)
XLA Modules:
  0.0 19.9 jit_solution(3005325701961863306)
XLA Ops:
  0.0 17.5 %harmonics.1 = (bf16[256,32]{1,0:T(8,128)(2,1)S(1)}, bf16[32,8192]{1,0:T(8,128)(2,1)S(1)}) custom-call(s32[16]{0:T(128)} %m_ref.1, bf16[1,32,1536]{2,1,0:T(8,128)(2,1)} %coeff_ref.1, bf16[1,1536,1536]{2,1,0:T(8,128)(2,1)} %blocks_ref.1, bf16[256,1536]{1,0:T(8,128)(2,1)} %bitcast.2), custom_call_target="tpu_custom_call" | custom-call | tf_op jit(solution)/shard_map/harmonics/pallas_call | solution.py:476
  17.6 2.3 %synthesis.1 = bf16[256,8192]{1,0:T(8,128)(2,1)} custom-call(bf16[256,32]{1,0:T(8,128)(2,1)S(1)} %get-tuple-element.7.h_v, bf16[32,8192]{1,0:T(8,128)(2,1)S(1)} %get-tuple-element.8.table), custom_call_target="tpu_custom_call" | custom-call | tf_op jit(solution)/shard_map/synthesis/pallas_call | solution.py:521
